TPU v7x, 32 devices: a whole 2x2x4 slice. The times are simulated.
32 devices in a mesh: row: 16 (over z, x, core), col: 2 (over y).
Axes of the slice: x: 2, y: 2, z: 4, core: 2. Of those that a mesh axis runs over, the one named last changes fastest.
Arguments:
- features: bfloat16 [16384, 256], P(('row', 'col')), may hold values from -6 to 6
- grad_out: bfloat16 [16384, 256], P(('row', 'col')), may hold values from -6 to 6
- weight: bfloat16 [256, 256], replicated, may hold values from -0.375 to 0.375
- tiles: bfloat16 [6144, 128, 128], P(('row', 'col')), may hold values from -0.125 to 0.125
- tile_row: int32 [6144], P(('row', 'col')), may hold values from 0 to 7
- tile_col: int32 [6144], P(('row', 'col')), may hold values from 0 to 63
- tile_count: int32 [32], P(('row', 'col')), may hold values from 24 to 192, as said below
Outputs:
- grad_features: bfloat16 [16384, 256], P(('row', 'col'))
- grad_weight: float32 [256, 256], replicated
Inputs may be any that keep to these rules, and one draw needn't show every extreme that they name: `tile_count`: exactly 192 on some device in every draw; slots of a device from its count on are not part of the adjacency.
All inputs are finite; a program needn't handle non-finite values.
Results may differ from a plain program's by a relative error of at most 0.02.
Values may be sent and summed in bfloat16 or wider, within the bound.
A program may use at most 128 MiB of HBM per device.

v0:
```python
import jax
import jax.numpy as jnp
from jax import lax
from jax.sharding import PartitionSpec as P


def silu_grad(preact, upstream):
    sigmoid_z = jax.nn.sigmoid(preact)
    return (upstream.astype(jnp.float32) * sigmoid_z * (1.0 + preact * (1.0 - sigmoid_z))).astype(
        jnp.bfloat16
    )


def spread_tiles(tiles, read_ids, write_ids, live_mask, panel, out_tiles, transpose):
    tile_size = tiles.shape[1]
    feat_width = panel.shape[-1]
    slots = tiles.shape[0]
    shaped = (
        tiles.reshape(4, slots // 4, tile_size, tile_size),
        read_ids.reshape(4, slots // 4),
        write_ids.reshape(4, slots // 4),
        live_mask.reshape(4, slots // 4),
    )
    form = "sji,sjf->sif" if transpose else "sij,sjf->sif"

    def step(total, block_data):
        part_tiles, read_part, write_part, live_part = block_data
        picked = panel[read_part]
        product = jnp.einsum(form, part_tiles, picked, preferred_element_type=jnp.float32)
        product = product * live_part.astype(jnp.float32)[:, None, None]
        return (total.at[write_part].add(product), None)

    start = jnp.zeros((out_tiles, tile_size, feat_width), jnp.float32)
    return lax.scan(step, start, shaped)[0]


def body(features, grad_out, weight, tiles, tile_row, tile_col, tile_count):
    segment = features.shape[0]
    feat_width = features.shape[1]
    tile_size = tiles.shape[1]
    mixed_rows = jnp.dot(features, weight, preferred_element_type=jnp.float32).astype(jnp.bfloat16)
    panel = lax.all_gather(mixed_rows, "row", axis=0, tiled=True)
    live_mask = jnp.arange(tile_row.shape[0], dtype=jnp.int32) < tile_count[0]
    col_tiles = panel.shape[0] // tile_size
    row_tiles = segment * lax.axis_size("col") // tile_size
    partial_value = spread_tiles(
        tiles,
        tile_col,
        tile_row,
        live_mask,
        panel.reshape(col_tiles, tile_size, feat_width),
        row_tiles,
        False,
    )
    partial_value = partial_value.reshape(row_tiles * tile_size, feat_width)
    owned = lax.psum_scatter(
        partial_value.astype(jnp.bfloat16), "col", scatter_dimension=0, tiled=True
    ).astype(jnp.float32)
    grad_block = lax.all_gather(silu_grad(owned, grad_out), "col", axis=0, tiled=True)
    back_terms = spread_tiles(
        tiles,
        tile_row,
        tile_col,
        live_mask,
        grad_block.reshape(row_tiles, tile_size, feat_width),
        col_tiles,
        True,
    )
    back_terms = back_terms.reshape(col_tiles * tile_size, feat_width).astype(jnp.bfloat16)
    summed = lax.psum_scatter(back_terms, "row", scatter_dimension=0, tiled=True).astype(
        jnp.float32
    )
    grad_panel = summed.astype(jnp.bfloat16)
    grad_features = lax.dot_general(
        grad_panel, weight, (((1,), (1,)), ((), ())), preferred_element_type=jnp.float32
    ).astype(jnp.bfloat16)
    local_weight = lax.dot_general(
        features, grad_panel, (((0,), (0,)), ((), ())), preferred_element_type=jnp.float32
    )
    grad_weight = lax.psum(local_weight, ("row", "col"))
    return (grad_features, grad_weight)


def solution(mesh):
    in_specs = (
        P(("row", "col"), None),
        P(("row", "col"), None),
        P(),
        P(("row", "col"), None, None),
        P(("row", "col")),
        P(("row", "col")),
        P(("row", "col")),
    )
    out_specs = (P(("row", "col"), None), P())
    return jax.shard_map(body, mesh=mesh, in_specs=in_specs, out_specs=out_specs, check_vma=False)
```

profile of v0, /device:TPU:0, one launch (start us, length us, event | category | flops | bytes accessed | tf_op | source)
XLA Modules:
  0.0 485.1 jit_solution(7939529680788866499)
XLA Ops:
  7.2 0.0 all-gather.2.cloned.1.call-start
  7.2 0.9 copy-done
  8.1 1.8 convolution_convert_fusion.1
  10.0 0.0 reduce-scatter.3.cloned.1.call-start
  10.7 0.8 reshape.157
  11.4 0.8 reshape.155
  12.2 51.6 %all-gather.2.cloned.1.call-done = bf16[8192,256]{1,0:T(8,128)(2,1)} async-done(((bf16[512,256]{1,0:T(8,128)(2,1)}), bf16[8192,256]{1,0:T(8,128)(2,1)}) %all-gather.2.cloned.1.call-update) | async-done | bytes 4194320 | tf_op jit(solution)/shard_map/all_gather | solution.py:42
  63.8 0.1 broadcast_in_dim.8
  63.9 81.0 %while.20 = (s32[]{:T(128)}, f32[8,128,256]{2,1,0:T(8,128)S(1)}, s32[4,48]{1,0:T(4,128)S(1)}, bf16[4,48,128,128]{3,2,1,0:T(8,128)(2,1)}, s32[4,48]{1,0:T(4,128)S...) while((s32[]{:T(128)}, f32[8,128,256]{2,1,0:T(8,128)S(1)}, ...), condition=%wide.region_2.3_spmd, body=%wide.region_0.2_spmd.sunk | while | flops 405800288 | bytes 36181848 | solution.py:34
  64.0 4.8 gather_fusion
  68.8 6.0 %broadcast_multiply_fusion.4 = f32[48,128,256]{2,1,0:T(8,128)} fusion(f32[48]{0:T(128)S(1)} %fusion.41, bf16[48,128,256]{2,1,0:T(8,128)(2,1)} %gather_fusion, bf16[4,48,128,128]{3,2,1,0:T(8,128)(2,1)} %get-tuple-element.232, s32[]{:T(128)S(6)} %copy.17), kind=kOutput, calls=%fused_computation.4.clone.1 | convolution fusion | flops 404226048 | bytes 11010244 | tf_op jit(solution)/shard_map/while/body/eval_jaxpr/sij,sjf->sif/dot_general | solution.py:29
  74.8 9.4 %scatter_fusion = f32[8,128,256]{2,1,0:T(8,128)S(1)} fusion(f32[8,128,256]{2,1,0:T(8,128)S(1)} %get-tuple-element.222, s32[48]{0:T(128)S(1)} %get-tuple-element.202, f32[48,128,256]{2,1,0:T(8,128)} %broadcast_multiply_fusion.4), kind=kCustom, calls=%fused_computation.2.clone.1 | custom fusion | flops 1572864 | bytes 18874560 | tf_op jit(solution)/shard_map/while/body/eval_jaxpr/scatter-add | solution.py:31
  84.2 4.8 gather_fusion
  89.0 6.0 %broadcast_multiply_fusion.4 = f32[48,128,256]{2,1,0:T(8,128)} fusion(f32[48]{0:T(128)S(1)} %fusion.41, bf16[48,128,256]{2,1,0:T(8,128)(2,1)} %gather_fusion, bf16[4,48,128,128]{3,2,1,0:T(8,128)(2,1)} %get-tuple-element.232, s32[]{:T(128)S(6)} %copy.17), kind=kOutput, calls=%fused_computation.4.clone.1 | convolution fusion | flops 404226048 | bytes 11010244 | tf_op jit(solution)/shard_map/while/body/eval_jaxpr/sij,sjf->sif/dot_general | solution.py:29
  95.0 9.4 %scatter_fusion = f32[8,128,256]{2,1,0:T(8,128)S(1)} fusion(f32[8,128,256]{2,1,0:T(8,128)S(1)} %get-tuple-element.222, s32[48]{0:T(128)S(1)} %get-tuple-element.202, f32[48,128,256]{2,1,0:T(8,128)} %broadcast_multiply_fusion.4), kind=kCustom, calls=%fused_computation.2.clone.1 | custom fusion | flops 1572864 | bytes 18874560 | tf_op jit(solution)/shard_map/while/body/eval_jaxpr/scatter-add | solution.py:31
  104.5 4.8 gather_fusion
  109.3 6.0 %broadcast_multiply_fusion.4 = f32[48,128,256]{2,1,0:T(8,128)} fusion(f32[48]{0:T(128)S(1)} %fusion.41, bf16[48,128,256]{2,1,0:T(8,128)(2,1)} %gather_fusion, bf16[4,48,128,128]{3,2,1,0:T(8,128)(2,1)} %get-tuple-element.232, s32[]{:T(128)S(6)} %copy.17), kind=kOutput, calls=%fused_computation.4.clone.1 | convolution fusion | flops 404226048 | bytes 11010244 | tf_op jit(solution)/shard_map/while/body/eval_jaxpr/sij,sjf->sif/dot_general | solution.py:29
  115.3 9.4 %scatter_fusion = f32[8,128,256]{2,1,0:T(8,128)S(1)} fusion(f32[8,128,256]{2,1,0:T(8,128)S(1)} %get-tuple-element.222, s32[48]{0:T(128)S(1)} %get-tuple-element.202, f32[48,128,256]{2,1,0:T(8,128)} %broadcast_multiply_fusion.4), kind=kCustom, calls=%fused_computation.2.clone.1 | custom fusion | flops 1572864 | bytes 18874560 | tf_op jit(solution)/shard_map/while/body/eval_jaxpr/scatter-add | solution.py:31
  124.8 4.8 gather_fusion
  129.5 6.0 %broadcast_multiply_fusion.4 = f32[48,128,256]{2,1,0:T(8,128)} fusion(f32[48]{0:T(128)S(1)} %fusion.41, bf16[48,128,256]{2,1,0:T(8,128)(2,1)} %gather_fusion, bf16[4,48,128,128]{3,2,1,0:T(8,128)(2,1)} %get-tuple-element.232, s32[]{:T(128)S(6)} %copy.17), kind=kOutput, calls=%fused_computation.4.clone.1 | convolution fusion | flops 404226048 | bytes 11010244 | tf_op jit(solution)/shard_map/while/body/eval_jaxpr/sij,sjf->sif/dot_general | solution.py:29
  135.5 9.4 %scatter_fusion = f32[8,128,256]{2,1,0:T(8,128)S(1)} fusion(f32[8,128,256]{2,1,0:T(8,128)S(1)} %get-tuple-element.222, s32[48]{0:T(128)S(1)} %get-tuple-element.202, f32[48,128,256]{2,1,0:T(8,128)} %broadcast_multiply_fusion.4), kind=kCustom, calls=%fused_computation.2.clone.1 | custom fusion | flops 1572864 | bytes 18874560 | tf_op jit(solution)/shard_map/while/body/eval_jaxpr/scatter-add | solution.py:31
  144.9 0.9 convert_element_type.51
  145.8 0.0 reduce-scatter.5.cloned.1.call-start
  145.9 8.7 %copy.9 = bf16[192,128,128]{1,2,0:T(8,128)(2,1)} copy(bf16[192,128,128]{2,1,0:T(8,128)(2,1)} %bitcast.83) | data formatting | bytes 12582912 | tf_op args[3]
  154.6 4.6 reduce-scatter.3.cloned.1.call-done
  159.1 1.2 fusion.21
  160.3 8.6 %all_gather.7 = bf16[1024,256]{1,0:T(8,128)(2,1)S(1)} all-gather(bf16[512,256]{1,0:T(8,128)(2,1)S(1)} %fusion.21), channel_id=1, replica_groups=mesh['row'=16,'col'=2] {'col'}, dimensions={0}, use_global_device_ids=true | all-gather | bytes 786432 | tf_op jit(solution)/shard_map/all_gather | solution.py:59
  168.9 4.2 broadcast_in_dim.4
  173.1 93.3 %while.21 = (s32[]{:T(128)}, f32[64,128,256]{2,1,0:T(8,128)}, s32[4,48]{1,0:T(4,128)S(1)}, bf16[4,48,128,128]{2,3,1,0:T(8,128)(2,1)}, s32[4,48]{1,0:T(4,128)S(1)...) while((s32[]{:T(128)}, f32[64,128,256]{2,1,0:T(8,128)}, ...), condition=%wide.region_6.7_spmd, body=%wide.region_4.6_spmd.sunk | while | flops 405800288 | bytes 36181848 | solution.py:34
  173.1 2.5 gather_fusion.1
  175.7 5.9 %broadcast_multiply_fusion.5 = f32[48,128,256]{2,1,0:T(8,128)} fusion(f32[48]{0:T(128)S(1)} %fusion.45, bf16[48,128,256]{2,1,0:T(8,128)(2,1)} %gather_fusion.1, bf16[4,48,128,128]{2,3,1,0:T(8,128)(2,1)} %get-tuple-element.256, s32[]{:T(128)S(6)} %copy.23), kind=kOutput, calls=%fused_computation.19.clone.1 | convolution fusion | flops 404226048 | bytes 11010244 | tf_op jit(solution)/shard_map/while/body/eval_jaxpr/sji,sjf->sif/dot_general | solution.py:29
  181.6 14.8 %scatter_fusion.1 = f32[64,128,256]{2,1,0:T(8,128)} fusion(f32[64,128,256]{2,1,0:T(8,128)} %get-tuple-element.246, s32[48]{0:T(128)S(1)} %get-tuple-element.211, f32[48,128,256]{2,1,0:T(8,128)} %broadcast_multiply_fusion.5), kind=kCustom, calls=%fused_computation.3.clone.1 | custom fusion | flops 1572864 | bytes 18874560 | tf_op jit(solution)/shard_map/while/body/eval_jaxpr/scatter-add | solution.py:31
  196.4 2.5 gather_fusion.1
  198.9 5.9 %broadcast_multiply_fusion.5 = f32[48,128,256]{2,1,0:T(8,128)} fusion(f32[48]{0:T(128)S(1)} %fusion.45, bf16[48,128,256]{2,1,0:T(8,128)(2,1)} %gather_fusion.1, bf16[4,48,128,128]{2,3,1,0:T(8,128)(2,1)} %get-tuple-element.256, s32[]{:T(128)S(6)} %copy.23), kind=kOutput, calls=%fused_computation.19.clone.1 | convolution fusion | flops 404226048 | bytes 11010244 | tf_op jit(solution)/shard_map/while/body/eval_jaxpr/sji,sjf->sif/dot_general | solution.py:29
  204.8 14.9 %scatter_fusion.1 = f32[64,128,256]{2,1,0:T(8,128)} fusion(f32[64,128,256]{2,1,0:T(8,128)} %get-tuple-element.246, s32[48]{0:T(128)S(1)} %get-tuple-element.211, f32[48,128,256]{2,1,0:T(8,128)} %broadcast_multiply_fusion.5), kind=kCustom, calls=%fused_computation.3.clone.1 | custom fusion | flops 1572864 | bytes 18874560 | tf_op jit(solution)/shard_map/while/body/eval_jaxpr/scatter-add | solution.py:31
  219.7 2.5 gather_fusion.1
  222.3 5.9 %broadcast_multiply_fusion.5 = f32[48,128,256]{2,1,0:T(8,128)} fusion(f32[48]{0:T(128)S(1)} %fusion.45, bf16[48,128,256]{2,1,0:T(8,128)(2,1)} %gather_fusion.1, bf16[4,48,128,128]{2,3,1,0:T(8,128)(2,1)} %get-tuple-element.256, s32[]{:T(128)S(6)} %copy.23), kind=kOutput, calls=%fused_computation.19.clone.1 | convolution fusion | flops 404226048 | bytes 11010244 | tf_op jit(solution)/shard_map/while/body/eval_jaxpr/sji,sjf->sif/dot_general | solution.py:29
  228.2 14.9 %scatter_fusion.1 = f32[64,128,256]{2,1,0:T(8,128)} fusion(f32[64,128,256]{2,1,0:T(8,128)} %get-tuple-element.246, s32[48]{0:T(128)S(1)} %get-tuple-element.211, f32[48,128,256]{2,1,0:T(8,128)} %broadcast_multiply_fusion.5), kind=kCustom, calls=%fused_computation.3.clone.1 | custom fusion | flops 1572864 | bytes 18874560 | tf_op jit(solution)/shard_map/while/body/eval_jaxpr/scatter-add | solution.py:31
  243.1 2.5 gather_fusion.1
  245.7 5.9 %broadcast_multiply_fusion.5 = f32[48,128,256]{2,1,0:T(8,128)} fusion(f32[48]{0:T(128)S(1)} %fusion.45, bf16[48,128,256]{2,1,0:T(8,128)(2,1)} %gather_fusion.1, bf16[4,48,128,128]{2,3,1,0:T(8,128)(2,1)} %get-tuple-element.256, s32[]{:T(128)S(6)} %copy.23), kind=kOutput, calls=%fused_computation.19.clone.1 | convolution fusion | flops 404226048 | bytes 11010244 | tf_op jit(solution)/shard_map/while/body/eval_jaxpr/sji,sjf->sif/dot_general | solution.py:29
  251.6 14.9 %scatter_fusion.1 = f32[64,128,256]{2,1,0:T(8,128)} fusion(f32[64,128,256]{2,1,0:T(8,128)} %get-tuple-element.246, s32[48]{0:T(128)S(1)} %get-tuple-element.211, f32[48,128,256]{2,1,0:T(8,128)} %broadcast_multiply_fusion.5), kind=kCustom, calls=%fused_computation.3.clone.1 | custom fusion | flops 1572864 | bytes 18874560 | tf_op jit(solution)/shard_map/while/body/eval_jaxpr/scatter-add | solution.py:31
  266.4 6.0 %convert_element_type.55 = bf16[64,128,256]{2,1,0:T(8,128)(2,1)} convert(f32[64,128,256]{2,1,0:T(8,128)} %get-tuple-element.77) | non-fusion elementwise | flops 2097152 | bytes 12582912 | tf_op jit(solution)/shard_map/convert_element_type | solution.py:69
  272.4 0.0 all-reduce.2.cloned.1.call-start
  272.5 72.7 %reduce-scatter.5.cloned.1.call-done = bf16[512,256]{1,0:T(8,128)(2,1)} async-done(((bf16[8192,256]{1,0:T(8,128)(2,1)}), bf16[512,256]{1,0:T(8,128)(2,1)}) %reduce-scatter.5.cloned.1.call-update) | async-done | bytes 262160 | tf_op jit(solution)/shard_map/reduce_scatter | solution.py:70
  345.2 1.9 convolution_bitcast_fusion
  347.1 1.9 convolution_convert_fusion
  349.1 127.8 %all-reduce.2.cloned.1.call-done = f32[256,256]{0,1:T(8,128)} async-done(((f32[256,256]{0,1:T(8,128)}), f32[256,256]{0,1:T(8,128)}) %all-reduce.2.cloned.1.call-update) | async-done | bytes 262160 | tf_op jit(solution)/shard_map/psum | solution.py:80
  476.8 1.8 copy.11
  (34 shorter events, 0.3 us)
Async XLA Ops:
  7.2 1.0 copy-start
  7.2 56.7 %all-gather.2.cloned.1.call-start = ((), (), s32[]{:S(2)}) async-start(), calls=%async_computation.2 | async-start | bytes 4456448 | tf_op jit(solution)/shard_map/all_gather | solution.py:42
  10.0 149.2 %reduce-scatter.3.cloned.1.call-start = ((), (), s32[]{:S(2)}) async-start(), calls=%async_computation.3 | async-start | bytes 786432 | tf_op jit(solution)/shard_map/reduce_scatter | solution.py:56
  145.8 13.3 %copy-start.2 = (bf16[512,256]{1,0:T(8,128)(2,1)S(1)}, bf16[512,256]{1,0:T(8,128)(2,1)}, u32[]{:S(2)}) copy-start(bf16[512,256]{1,0:T(8,128)(2,1)} %param.12) | copy-start | bytes 786436
  145.8 199.4 %reduce-scatter.5.cloned.1.call-start = ((), (), s32[]{:S(2)}) async-start(), calls=%async_computation.4 | async-start | bytes 4456448 | tf_op jit(solution)/shard_map/reduce_scatter | solution.py:70
  266.4 80.7 %copy-start.1 = (bf16[256,256]{1,0:T(8,128)(2,1)S(1)}, bf16[256,256]{1,0:T(8,128)(2,1)}, u32[]{:S(2)}) copy-start(bf16[256,256]{1,0:T(8,128)(2,1)} %param.13) | copy-start | bytes 393220
  272.4 204.4 %all-reduce.2.cloned.1.call-start = ((), (), s32[]{:S(2)}) async-start(), calls=%async_computation.5 | async-start | bytes 524288 | tf_op jit(solution)/shard_map/psum | solution.py:80
Sparse Core Ops, SparseCore 0:
  10.7 53.0 all-gather.1
  145.9 13.1 reduce-scatter.2
  272.6 72.5 reduce-scatter.4
  351.1 125.6 all-reduce.1
where the time goes:
time: 486 us; the launch traced here: 485 us
  waiting for transfers between devices  257 us (53%)
  other arithmetic  105 us (22%)
  matrix products  53.2 us (11%)
  local copies, waits for them, and re-layouts  46.5 us (10%)
  between operations  14.5 us (3%)
  blocking collectives  8.55 us (2%)
    psum x1, waiting for transfers between devices, body(): grad_weight = lax.psum(local_weight, ('row', 'col'))  128 us
    scatter-add x8, other arithmetic, step(): return (total.at[write_part].add(product), None)  97.1 us
    reduce_scatter x1, waiting for transfers between devices, body(): lax.psum_scatter(back_terms, 'row', scatter_dimension=0, tiled=True)  72.7 us
    all_gather x1, waiting for transfers between devices, body(): panel = lax.all_gather(mixed_rows, 'row', axis=0, tiled=True)  51.6 us
    dot_general x8, matrix products, step(): jnp.einsum(form, part_tiles, picked, preferred_element_type=jnp.float32)  47.5 us
    gather x8, local copies, waits for them, and re-layouts, step(): picked = panel[read_part]  29.3 us
    unnamed x8, local copies, waits for them, and re-layouts  11.4 us
  transfers between devices with their start and end apart: 4, of which 4 were waited for; matrix products, arithmetic and copies ran while one was open for 2% of the time, Pallas kernels for 0%

commit v1 on v0

--- a/solution.py
+++ b/solution.py
@@ -77,7 +77,7 @@
     local_weight = lax.dot_general(
         features, grad_panel, (((0,), (0,)), ((), ())), preferred_element_type=jnp.float32
     )
-    grad_weight = lax.psum(local_weight, ("row", "col"))
+    grad_weight = jnp.sum(lax.all_gather(local_weight, ("row", "col")), axis=0)
     return (grad_features, grad_weight)
 
 

time: 486 us -> 449 us (0.924)
  waiting for transfers between devices: 257 us -> 211 us
  local copies, waits for them, and re-layouts: 46.5 us -> 52.4 us
    psum x1 -> x0, waiting for transfers between devices: 128 us -> none  [body(): grad_weight = lax.psum(local_weight, ('row', 'col'))]
    all_gather x0 -> x1, waiting for transfers between devices: none -> 82.6 us  [body(): grad_weight = jnp.sum(lax.all_gather(local_weight, ('row', 'col')), axis=0)]
    unnamed x8 -> x9, local copies, waits for them, and re-layouts: 11.4 us -> 17.3 us
  transfers between devices with their start and end apart: 4 -> 4, of which waited for: 4 -> 4; matrix products, arithmetic and copies ran while one was open for 2% -> 3% of each run, Pallas kernels for 0% -> 0%
where the time goes in v1:
time: 449 us; the launch traced here: 448 us
  waiting for transfers between devices  211 us (47%)
  other arithmetic  107 us (24%)
  matrix products  53.2 us (12%)
  local copies, waits for them, and re-layouts  52.4 us (12%)
  between operations  14.5 us (3%)
  blocking collectives  8.53 us (2%)
    scatter-add x8, other arithmetic, step(): return (total.at[write_part].add(product), None)  97.1 us
    all_gather x1, waiting for transfers between devices, body(): grad_weight = jnp.sum(lax.all_gather(local_weight, ('row', 'col')), axis=0)  82.6 us
    reduce_scatter x1, waiting for transfers between devices, body(): lax.psum_scatter(back_terms, 'row', scatter_dimension=0, tiled=True)  72.5 us
    all_gather x1, waiting for transfers between devices, body(): panel = lax.all_gather(mixed_rows, 'row', axis=0, tiled=True)  51.6 us
    dot_general x8, matrix products, step(): jnp.einsum(form, part_tiles, picked, preferred_element_type=jnp.float32)  47.5 us
    gather x8, local copies, waits for them, and re-layouts, step(): picked = panel[read_part]  29.3 us
    unnamed x9, local copies, waits for them, and re-layouts  17.3 us
  transfers between devices with their start and end apart: 4, of which 4 were waited for; matrix products, arithmetic and copies ran while one was open for 3% of the time, Pallas kernels for 0%

profile of v1, /device:TPU:0, one launch (start us, length us, event | category | flops | bytes accessed | tf_op | source)
XLA Modules:
  0.0 447.8 jit_solution(4752558002948924625)
XLA Ops:
  7.2 0.9 copy-done
  8.1 1.8 convolution_convert_fusion.1
  10.0 0.0 reduce-scatter.3.cloned.1.call-start
  10.7 0.8 reshape.157
  11.4 0.8 reshape.155
  12.2 51.6 %all-gather.4.cloned.1.call-done = bf16[8192,256]{1,0:T(8,128)(2,1)} async-done(((bf16[512,256]{1,0:T(8,128)(2,1)}), bf16[8192,256]{1,0:T(8,128)(2,1)}) %all-gather.4.cloned.1.call-update) | async-done | bytes 4194320 | tf_op jit(solution)/shard_map/all_gather | solution.py:42
  63.8 0.1 broadcast_in_dim.8
  63.9 81.0 %while.20 = (s32[]{:T(128)}, f32[8,128,256]{2,1,0:T(8,128)S(1)}, s32[4,48]{1,0:T(4,128)S(1)}, bf16[4,48,128,128]{3,2,1,0:T(8,128)(2,1)}, s32[4,48]{1,0:T(4,128)S...) while((s32[]{:T(128)}, f32[8,128,256]{2,1,0:T(8,128)S(1)}, ...), condition=%wide.region_2.3_spmd, body=%wide.region_0.2_spmd.sunk | while | flops 405800288 | bytes 36181848 | solution.py:34
  64.0 4.8 %gather_fusion = bf16[48,128,256]{2,1,0:T(8,128)(2,1)} fusion(bf16[64,128,256]{2,1,0:T(8,128)(2,1)} %get-tuple-element.241, s32[1024]{0:T(1024)S(1)} %pad_clamp_fusion.4), kind=kCustom, calls=%fused_computation.clone.1 | custom fusion | bytes 6291648 | tf_op jit(solution)/shard_map/while/body/eval_jaxpr/gather | solution.py:28
  68.8 6.0 %broadcast_multiply_fusion.4 = f32[48,128,256]{2,1,0:T(8,128)} fusion(f32[48]{0:T(128)S(1)} %fusion.41, bf16[48,128,256]{2,1,0:T(8,128)(2,1)} %gather_fusion, bf16[4,48,128,128]{3,2,1,0:T(8,128)(2,1)} %get-tuple-element.239, s32[]{:T(128)S(6)} %copy.20), kind=kOutput, calls=%fused_computation.4.clone.1 | convolution fusion | flops 404226048 | bytes 11010244 | tf_op jit(solution)/shard_map/while/body/eval_jaxpr/sij,sjf->sif/dot_general | solution.py:29
  74.8 9.4 %scatter_fusion = f32[8,128,256]{2,1,0:T(8,128)S(1)} fusion(f32[8,128,256]{2,1,0:T(8,128)S(1)} %get-tuple-element.229, s32[48]{0:T(128)S(1)} %get-tuple-element.209, f32[48,128,256]{2,1,0:T(8,128)} %broadcast_multiply_fusion.4), kind=kCustom, calls=%fused_computation.2.clone.1 | custom fusion | flops 1572864 | bytes 18874560 | tf_op jit(solution)/shard_map/while/body/eval_jaxpr/scatter-add | solution.py:31
  84.2 4.8 %gather_fusion = bf16[48,128,256]{2,1,0:T(8,128)(2,1)} fusion(bf16[64,128,256]{2,1,0:T(8,128)(2,1)} %get-tuple-element.241, s32[1024]{0:T(1024)S(1)} %pad_clamp_fusion.4), kind=kCustom, calls=%fused_computation.clone.1 | custom fusion | bytes 6291648 | tf_op jit(solution)/shard_map/while/body/eval_jaxpr/gather | solution.py:28
  89.0 6.0 %broadcast_multiply_fusion.4 = f32[48,128,256]{2,1,0:T(8,128)} fusion(f32[48]{0:T(128)S(1)} %fusion.41, bf16[48,128,256]{2,1,0:T(8,128)(2,1)} %gather_fusion, bf16[4,48,128,128]{3,2,1,0:T(8,128)(2,1)} %get-tuple-element.239, s32[]{:T(128)S(6)} %copy.20), kind=kOutput, calls=%fused_computation.4.clone.1 | convolution fusion | flops 404226048 | bytes 11010244 | tf_op jit(solution)/shard_map/while/body/eval_jaxpr/sij,sjf->sif/dot_general | solution.py:29
  95.0 9.4 %scatter_fusion = f32[8,128,256]{2,1,0:T(8,128)S(1)} fusion(f32[8,128,256]{2,1,0:T(8,128)S(1)} %get-tuple-element.229, s32[48]{0:T(128)S(1)} %get-tuple-element.209, f32[48,128,256]{2,1,0:T(8,128)} %broadcast_multiply_fusion.4), kind=kCustom, calls=%fused_computation.2.clone.1 | custom fusion | flops 1572864 | bytes 18874560 | tf_op jit(solution)/shard_map/while/body/eval_jaxpr/scatter-add | solution.py:31
  104.5 4.8 %gather_fusion = bf16[48,128,256]{2,1,0:T(8,128)(2,1)} fusion(bf16[64,128,256]{2,1,0:T(8,128)(2,1)} %get-tuple-element.241, s32[1024]{0:T(1024)S(1)} %pad_clamp_fusion.4), kind=kCustom, calls=%fused_computation.clone.1 | custom fusion | bytes 6291648 | tf_op jit(solution)/shard_map/while/body/eval_jaxpr/gather | solution.py:28
  109.3 6.0 %broadcast_multiply_fusion.4 = f32[48,128,256]{2,1,0:T(8,128)} fusion(f32[48]{0:T(128)S(1)} %fusion.41, bf16[48,128,256]{2,1,0:T(8,128)(2,1)} %gather_fusion, bf16[4,48,128,128]{3,2,1,0:T(8,128)(2,1)} %get-tuple-element.239, s32[]{:T(128)S(6)} %copy.20), kind=kOutput, calls=%fused_computation.4.clone.1 | convolution fusion | flops 404226048 | bytes 11010244 | tf_op jit(solution)/shard_map/while/body/eval_jaxpr/sij,sjf->sif/dot_general | solution.py:29
  115.3 9.4 %scatter_fusion = f32[8,128,256]{2,1,0:T(8,128)S(1)} fusion(f32[8,128,256]{2,1,0:T(8,128)S(1)} %get-tuple-element.229, s32[48]{0:T(128)S(1)} %get-tuple-element.209, f32[48,128,256]{2,1,0:T(8,128)} %broadcast_multiply_fusion.4), kind=kCustom, calls=%fused_computation.2.clone.1 | custom fusion | flops 1572864 | bytes 18874560 | tf_op jit(solution)/shard_map/while/body/eval_jaxpr/scatter-add | solution.py:31
  124.7 4.8 %gather_fusion = bf16[48,128,256]{2,1,0:T(8,128)(2,1)} fusion(bf16[64,128,256]{2,1,0:T(8,128)(2,1)} %get-tuple-element.241, s32[1024]{0:T(1024)S(1)} %pad_clamp_fusion.4), kind=kCustom, calls=%fused_computation.clone.1 | custom fusion | bytes 6291648 | tf_op jit(solution)/shard_map/while/body/eval_jaxpr/gather | solution.py:28
  129.5 6.0 %broadcast_multiply_fusion.4 = f32[48,128,256]{2,1,0:T(8,128)} fusion(f32[48]{0:T(128)S(1)} %fusion.41, bf16[48,128,256]{2,1,0:T(8,128)(2,1)} %gather_fusion, bf16[4,48,128,128]{3,2,1,0:T(8,128)(2,1)} %get-tuple-element.239, s32[]{:T(128)S(6)} %copy.20), kind=kOutput, calls=%fused_computation.4.clone.1 | convolution fusion | flops 404226048 | bytes 11010244 | tf_op jit(solution)/shard_map/while/body/eval_jaxpr/sij,sjf->sif/dot_general | solution.py:29
  135.5 9.4 %scatter_fusion = f32[8,128,256]{2,1,0:T(8,128)S(1)} fusion(f32[8,128,256]{2,1,0:T(8,128)S(1)} %get-tuple-element.229, s32[48]{0:T(128)S(1)} %get-tuple-element.209, f32[48,128,256]{2,1,0:T(8,128)} %broadcast_multiply_fusion.4), kind=kCustom, calls=%fused_computation.2.clone.1 | custom fusion | flops 1572864 | bytes 18874560 | tf_op jit(solution)/shard_map/while/body/eval_jaxpr/scatter-add | solution.py:31
  144.9 0.9 convert_element_type.51
  145.9 8.7 %copy.11 = bf16[192,128,128]{1,2,0:T(8,128)(2,1)} copy(bf16[192,128,128]{2,1,0:T(8,128)(2,1)} %bitcast.88) | data formatting | bytes 12582912 | tf_op args[3]
  154.6 4.6 %reduce-scatter.3.cloned.1.call-done = bf16[512,256]{1,0:T(8,128)(2,1)} async-done(((bf16[1024,256]{1,0:T(8,128)(2,1)}), bf16[512,256]{1,0:T(8,128)(2,1)}) %reduce-scatter.3.cloned.1.call-update) | async-done | bytes 262160 | tf_op jit(solution)/shard_map/reduce_scatter | solution.py:56
  159.1 1.2 fusion.21
  160.3 8.5 %all_gather.13 = bf16[1024,256]{1,0:T(8,128)(2,1)S(1)} all-gather(bf16[512,256]{1,0:T(8,128)(2,1)S(1)} %fusion.21), channel_id=1, replica_groups=mesh['row'=16,'col'=2] {'col'}, dimensions={0}, use_global_device_ids=true | all-gather | bytes 786432 | tf_op jit(solution)/shard_map/all_gather | solution.py:59
  168.8 4.2 broadcast_in_dim.4
  173.1 93.3 %while.21 = (s32[]{:T(128)}, f32[64,128,256]{2,1,0:T(8,128)}, s32[4,48]{1,0:T(4,128)S(1)}, bf16[4,48,128,128]{2,3,1,0:T(8,128)(2,1)}, s32[4,48]{1,0:T(4,128)S(1)...) while((s32[]{:T(128)}, f32[64,128,256]{2,1,0:T(8,128)}, ...), condition=%wide.region_6.7_spmd, body=%wide.region_4.6_spmd.sunk | while | flops 405800288 | bytes 36181848 | solution.py:34
  173.1 2.5 gather_fusion.1
  175.7 5.9 %broadcast_multiply_fusion.5 = f32[48,128,256]{2,1,0:T(8,128)} fusion(f32[48]{0:T(128)S(1)} %fusion.45, bf16[48,128,256]{2,1,0:T(8,128)(2,1)} %gather_fusion.1, bf16[4,48,128,128]{2,3,1,0:T(8,128)(2,1)} %get-tuple-element.263, s32[]{:T(128)S(6)} %copy.26), kind=kOutput, calls=%fused_computation.19.clone.1 | convolution fusion | flops 404226048 | bytes 11010244 | tf_op jit(solution)/shard_map/while/body/eval_jaxpr/sji,sjf->sif/dot_general | solution.py:29
  181.6 14.8 %scatter_fusion.1 = f32[64,128,256]{2,1,0:T(8,128)} fusion(f32[64,128,256]{2,1,0:T(8,128)} %get-tuple-element.253, s32[48]{0:T(128)S(1)} %get-tuple-element.218, f32[48,128,256]{2,1,0:T(8,128)} %broadcast_multiply_fusion.5), kind=kCustom, calls=%fused_computation.3.clone.1 | custom fusion | flops 1572864 | bytes 18874560 | tf_op jit(solution)/shard_map/while/body/eval_jaxpr/scatter-add | solution.py:31
  196.4 2.5 gather_fusion.1
  198.9 5.9 %broadcast_multiply_fusion.5 = f32[48,128,256]{2,1,0:T(8,128)} fusion(f32[48]{0:T(128)S(1)} %fusion.45, bf16[48,128,256]{2,1,0:T(8,128)(2,1)} %gather_fusion.1, bf16[4,48,128,128]{2,3,1,0:T(8,128)(2,1)} %get-tuple-element.263, s32[]{:T(128)S(6)} %copy.26), kind=kOutput, calls=%fused_computation.19.clone.1 | convolution fusion | flops 404226048 | bytes 11010244 | tf_op jit(solution)/shard_map/while/body/eval_jaxpr/sji,sjf->sif/dot_general | solution.py:29
  204.8 14.9 %scatter_fusion.1 = f32[64,128,256]{2,1,0:T(8,128)} fusion(f32[64,128,256]{2,1,0:T(8,128)} %get-tuple-element.253, s32[48]{0:T(128)S(1)} %get-tuple-element.218, f32[48,128,256]{2,1,0:T(8,128)} %broadcast_multiply_fusion.5), kind=kCustom, calls=%fused_computation.3.clone.1 | custom fusion | flops 1572864 | bytes 18874560 | tf_op jit(solution)/shard_map/while/body/eval_jaxpr/scatter-add | solution.py:31
  219.7 2.5 gather_fusion.1
  222.3 5.9 %broadcast_multiply_fusion.5 = f32[48,128,256]{2,1,0:T(8,128)} fusion(f32[48]{0:T(128)S(1)} %fusion.45, bf16[48,128,256]{2,1,0:T(8,128)(2,1)} %gather_fusion.1, bf16[4,48,128,128]{2,3,1,0:T(8,128)(2,1)} %get-tuple-element.263, s32[]{:T(128)S(6)} %copy.26), kind=kOutput, calls=%fused_computation.19.clone.1 | convolution fusion | flops 404226048 | bytes 11010244 | tf_op jit(solution)/shard_map/while/body/eval_jaxpr/sji,sjf->sif/dot_general | solution.py:29
  228.2 14.9 %scatter_fusion.1 = f32[64,128,256]{2,1,0:T(8,128)} fusion(f32[64,128,256]{2,1,0:T(8,128)} %get-tuple-element.253, s32[48]{0:T(128)S(1)} %get-tuple-element.218, f32[48,128,256]{2,1,0:T(8,128)} %broadcast_multiply_fusion.5), kind=kCustom, calls=%fused_computation.3.clone.1 | custom fusion | flops 1572864 | bytes 18874560 | tf_op jit(solution)/shard_map/while/body/eval_jaxpr/scatter-add | solution.py:31
  243.1 2.5 gather_fusion.1
  245.6 5.9 %broadcast_multiply_fusion.5 = f32[48,128,256]{2,1,0:T(8,128)} fusion(f32[48]{0:T(128)S(1)} %fusion.45, bf16[48,128,256]{2,1,0:T(8,128)(2,1)} %gather_fusion.1, bf16[4,48,128,128]{2,3,1,0:T(8,128)(2,1)} %get-tuple-element.263, s32[]{:T(128)S(6)} %copy.26), kind=kOutput, calls=%fused_computation.19.clone.1 | convolution fusion | flops 404226048 | bytes 11010244 | tf_op jit(solution)/shard_map/while/body/eval_jaxpr/sji,sjf->sif/dot_general | solution.py:29
  251.5 14.9 %scatter_fusion.1 = f32[64,128,256]{2,1,0:T(8,128)} fusion(f32[64,128,256]{2,1,0:T(8,128)} %get-tuple-element.253, s32[48]{0:T(128)S(1)} %get-tuple-element.218, f32[48,128,256]{2,1,0:T(8,128)} %broadcast_multiply_fusion.5), kind=kCustom, calls=%fused_computation.3.clone.1 | custom fusion | flops 1572864 | bytes 18874560 | tf_op jit(solution)/shard_map/while/body/eval_jaxpr/scatter-add | solution.py:31
  266.4 6.0 %convert_element_type.55 = bf16[64,128,256]{2,1,0:T(8,128)(2,1)} convert(f32[64,128,256]{2,1,0:T(8,128)} %get-tuple-element.77) | non-fusion elementwise | flops 2097152 | bytes 12582912 | tf_op jit(solution)/shard_map/convert_element_type | solution.py:69
  272.4 0.2 all-gather.6.cloned.1.call-start
  272.6 72.5 %reduce-scatter.5.cloned.1.call-done = bf16[512,256]{1,0:T(8,128)(2,1)} async-done(((bf16[8192,256]{1,0:T(8,128)(2,1)}), bf16[512,256]{1,0:T(8,128)(2,1)}) %reduce-scatter.5.cloned.1.call-update) | async-done | bytes 262160 | tf_op jit(solution)/shard_map/reduce_scatter | solution.py:70
  345.2 1.9 convolution_bitcast_fusion
  347.1 1.9 convolution_convert_fusion
  349.1 82.6 %all-gather.6.cloned.1.call-done = f32[8192,256]{0,1:T(8,128)} async-done(((f32[256,256]{0,1:T(8,128)}), f32[8192,256]{0,1:T(8,128)}) %all-gather.6.cloned.1.call-update) | async-done | bytes 8388624 | tf_op jit(solution)/shard_map/all_gather | solution.py:80
  431.6 6.8 %copy.15 = f32[32,8,32,256]{3,2,1,0:T(8,128)S(1)} copy(f32[32,8,32,256]{3,1,2,0:T(8,128)} %bitcast.91) | data formatting | bytes 16777216
  438.5 1.9 bitcast_reduce_fusion
  440.4 0.8 copy.13
  (36 shorter events, 0.4 us)
Async XLA Ops:
  7.2 1.0 copy-start
  7.2 56.7 %all-gather.4.cloned.1.call-start = ((), (), s32[]{:S(2)}) async-start(), calls=%async_computation.2 | async-start | bytes 4456448 | tf_op jit(solution)/shard_map/all_gather | solution.py:42
  10.0 149.2 %reduce-scatter.3.cloned.1.call-start = ((), (), s32[]{:S(2)}) async-start(), calls=%async_computation.3 | async-start | bytes 786432 | tf_op jit(solution)/shard_map/reduce_scatter | solution.py:56
  145.8 13.3 %copy-start.2 = (bf16[512,256]{1,0:T(8,128)(2,1)S(1)}, bf16[512,256]{1,0:T(8,128)(2,1)}, u32[]{:S(2)}) copy-start(bf16[512,256]{1,0:T(8,128)(2,1)} %param.12) | copy-start | bytes 786436
  145.8 199.4 %reduce-scatter.5.cloned.1.call-start = ((), (), s32[]{:S(2)}) async-start(), calls=%async_computation.4 | async-start | bytes 4456448 | tf_op jit(solution)/shard_map/reduce_scatter | solution.py:70
  266.4 80.7 %copy-start.1 = (bf16[256,256]{1,0:T(8,128)(2,1)S(1)}, bf16[256,256]{1,0:T(8,128)(2,1)}, u32[]{:S(2)}) copy-start(bf16[256,256]{1,0:T(8,128)(2,1)} %param.13) | copy-start | bytes 393220
  272.4 159.2 %all-gather.6.cloned.1.call-start = ((), (), s32[]{:S(2)}) async-start(), calls=%async_computation.5 | async-start | bytes 8650752 | tf_op jit(solution)/shard_map/all_gather | solution.py:80
Sparse Core Ops, SparseCore 0:
  10.7 53.0 all-gather.3
  145.9 13.1 reduce-scatter.2
  272.5 72.6 reduce-scatter.4
  348.5 83.0 all-gather.5
